TPU v7x, 256 devices: a whole 4x4x8 slice. The times are simulated.
256 devices in a mesh: replica: 8 (over z_lo, x), fsdp: 32 (over z_hi, y, core).
Axes of the slice: x: 4, y: 4, z: 8 (z_hi: 4, z_lo: 2; z = z_hi * 2 + z_lo), core: 2. Of those that a mesh axis runs over, the one named last changes fastest.
Arguments:
- counts: int32 [8], P('replica'), may hold values from 100 to 1000
- inner: bfloat16 [8, 3, 2, 8192, 1024], P('replica', None, None, 'fsdp'), may hold values from -6 to 6
- anchor: bfloat16 [3, 2, 8192, 1024], P(None, None, 'fsdp'), may hold values from -6 to 6
- momentum: float32 [3, 2, 8192, 1024], P(None, None, ('fsdp', 'replica')), may hold values from -6 to 6
Outputs:
- new_weights: bfloat16 [3, 2, 8192, 1024], P(None, None, 'fsdp')
- new_momentum: float32 [3, 2, 8192, 1024], P(None, None, ('fsdp', 'replica'))
Inputs may be any that keep to these rules, and one draw needn't show every extreme that they name: `counts`: inner steps of a group.
All inputs are finite; a program needn't handle non-finite values.
Results may differ from a plain program's by a relative error of at most 0.001.
Values may be sent and summed in bfloat16 or wider, within the bound.
A program may use at most 128 MiB of HBM per device.

v0:
```python
import jax
import jax.numpy as jnp
from jax import lax
from jax.sharding import PartitionSpec as P

LAYERS = 3
outer_rate = 0.7
momentum_rate = 0.9


def on_device(counts, inner, anchor, momentum):
    total = lax.psum(counts[0], "replica").astype(jnp.float32)
    share = counts[0].astype(jnp.float32) / total
    owned_rows = momentum.shape[2]
    start = lax.axis_index("replica") * owned_rows
    weight_list = []
    moment_list = []
    for layer in range(LAYERS):
        base = anchor[layer].astype(jnp.float32)
        term = share * (base - inner[0, layer].astype(jnp.float32))
        pseudo = lax.psum(term, "replica")
        moment_full = lax.all_gather(momentum[layer], "replica", axis=1, tiled=True)
        moment_next = momentum_rate * moment_full + pseudo
        weights_next = (base - outer_rate * (pseudo + momentum_rate * moment_next)).astype(
            jnp.bfloat16
        )
        moment_list.append(lax.dynamic_slice_in_dim(moment_next, start, owned_rows, 1))
        weight_list.append(weights_next)
    return (jnp.stack(weight_list), jnp.stack(moment_list))


def solution(mesh):
    placed = (
        P("replica"),
        P("replica", None, None, "fsdp", None),
        P(None, None, "fsdp", None),
        P(None, None, ("fsdp", "replica"), None),
    )
    return jax.shard_map(
        on_device,
        mesh=mesh,
        in_specs=placed,
        out_specs=(P(None, None, "fsdp", None), P(None, None, ("fsdp", "replica"), None)),
        check_vma=False,
    )
```

profile of v0, /device:TPU:8, one launch (start us, length us, event | category | flops | bytes accessed | tf_op | source)
XLA Modules:
  0.0 314.4 jit_solution(1849387459540233903)
XLA Ops:
  7.2 0.0 all-gather.11.cloned.1.call-start
  7.2 2.0 fusion.9
  9.2 0.0 all-gather.11.cloned.1.call-update
  9.2 0.0 all-reduce.3.cloned.1.call-start
  9.3 13.1 %psum.28 = s32[]{:T(128)} all-reduce(s32[]{:T(128)} %bitcast.1), channel_id=1, replica_groups=mesh['replica'=8,'fsdp'=32] {'replica'}, use_global_device_ids=true, to_apply=%region_0.0 | all-reduce | flops 1 | bytes 8 | tf_op jit(solution)/shard_map/psum | solution.py:12
  23.8 6.1 %fusion = (f32[2,256,1024]{2,1,0:T(8,128)}, f32[2,256,1024]{2,1,0:T(8,128)}, f32[2,256,1024]{2,1,0:T(8,128)}) fusion(bf16[1,3,2,256,1024]{4,3,2,1,0:T(8,128)(2,1)} %param.5, f32[]{:T(128)S(6)} %div.3, bf16[3,2,256,1024]{3,2,1,0:T(8,128)(2,1)} %param.6), kind=kLoop, calls=%fused_computation.7 | loop fusion | flops 6291456 | bytes 12582916 | tf_op jit(solution)/shard_map/mul | solution.py:20
  29.9 0.0 copy-start
  29.9 0.0 all-reduce.3.cloned.1.call-update
  29.9 0.0 all-gather.9.cloned.1.call-start
  30.0 0.7 all-gather.9.cloned.1.call-update
  30.7 0.0 all-gather.7.cloned.1.call-start
  30.7 0.5 all-gather.7.cloned.1.call-update
  31.3 25.7 %all-gather.11.cloned.1.call-done = f32[1,2,256,1024]{3,2,1,0:T(8,128)} async-done(((f32[1,2,32,1024]{3,2,1,0:T(8,128)}), f32[1,2,256,1024]{3,2,1,0:T(8,128)}) %all-gather.11.cloned.1.call-update) | async-done | bytes 2097168 | tf_op jit(solution)/shard_map/all_gather | solution.py:22
  57.0 153.2 %all-reduce.3.cloned.1.call-done = (f32[2,256,1024]{2,1,0:T(8,128)}, f32[2,256,1024]{2,1,0:T(8,128)}, f32[2,256,1024]{2,1,0:T(8,128)}) async-done(((f32[2,256,1024]{2,1,0:T(8,128)}, f32[2,256,1024]{2,1,0:T(8,128)}, f32[2,256,1024]{2,1,0:T(8,128)}), (f32[2,256,1024]{2,1,0:T(8,128)}, f32[2,256,1024]{2,1,0:T(8,128)}, f32[2,256,1024]{2,1,0:T(8,128)})) %all-reduce.3.cloned.1.call-update) | async-done | bytes 6291472 | tf_op jit(solution)/shard_map/psum | solution.py:21
  210.2 0.0 copy-done
  210.2 3.8 %bitcast_add_fusion = (f32[2,256,1024]{2,1,0:T(8,128)S(1)}, bf16[1,2,256,1024]{3,2,1,0:T(8,128)(2,1)}) fusion(f32[2,256,1024]{2,1,0:T(8,128)} %get-tuple-element.2, f32[1,2,256,1024]{3,2,1,0:T(8,128)} %all-gather.11.cloned.1.call-done, bf16[3,2,256,1024]{3,2,1,0:T(8,128)(2,1)S(1)} %copy-done), kind=kLoop, calls=%fused_computation.13 | loop fusion | flops 4194304 | bytes 8388608 | tf_op jit(solution)/shard_map/add | solution.py:23
  214.1 41.2 %all-gather.9.cloned.1.call-done = f32[1,2,256,1024]{3,2,1,0:T(8,128)} async-done(((f32[1,2,32,1024]{3,2,1,0:T(8,128)}), f32[1,2,256,1024]{3,2,1,0:T(8,128)}) %all-gather.9.cloned.1.call-update) | async-done | bytes 2097168 | tf_op jit(solution)/shard_map/all_gather | solution.py:22
  255.3 3.9 %bitcast_add_fusion.1 = (f32[2,256,1024]{2,1,0:T(8,128)S(1)}, bf16[1,2,256,1024]{3,2,1,0:T(8,128)(2,1)}) fusion(f32[2,256,1024]{2,1,0:T(8,128)} %get-tuple-element.3, f32[1,2,256,1024]{3,2,1,0:T(8,128)} %all-gather.9.cloned.1.call-done, bf16[3,2,256,1024]{3,2,1,0:T(8,128)(2,1)S(1)} %copy-done), kind=kLoop, calls=%fused_computation.14 | loop fusion | flops 4194304 | bytes 8388608 | tf_op jit(solution)/shard_map/add | solution.py:23
  259.1 0.7 dynamic-slice_bitcast_fusion.1
  259.9 41.0 %all-gather.7.cloned.1.call-done = f32[1,2,256,1024]{3,2,1,0:T(8,128)} async-done(((f32[1,2,32,1024]{3,2,1,0:T(8,128)}), f32[1,2,256,1024]{3,2,1,0:T(8,128)}) %all-gather.7.cloned.1.call-update) | async-done | bytes 2097168 | tf_op jit(solution)/shard_map/all_gather | solution.py:22
  300.9 0.0 copy-start.3
  300.9 3.1 bitcast_add_fusion.2
  304.0 0.0 copy-start.1
  304.0 0.0 copy-start.2
  304.1 0.0 copy-done.3
  304.1 0.9 pad_maximum_fusion.1
  305.0 0.5 copy-done.1
  305.5 0.3 copy-done.2
  305.8 2.0 pad_maximum_fusion
  (2 shorter events, 0.0 us)
Async XLA Ops:
  7.2 49.8 %all-gather.11.cloned.1.call-start = ((), (), s32[]{:S(2)}) async-start(), calls=%async_computation.2 | async-start | bytes 2359296 | tf_op jit(solution)/shard_map/all_gather | solution.py:22
  9.2 201.0 %all-reduce.3.cloned.1.call-start = ((), (), s32[]{:S(2)}) async-start(), calls=%async_computation.3 | async-start | bytes 12582912 | tf_op jit(solution)/shard_map/psum | solution.py:21
  29.9 180.3 %copy-start = (bf16[3,2,256,1024]{3,2,1,0:T(8,128)(2,1)S(1)}, bf16[3,2,256,1024]{3,2,1,0:T(8,128)(2,1)}, u32[]{:S(2)}) copy-start(bf16[3,2,256,1024]{3,2,1,0:T(8,128)(2,1)} %param.6) | copy-start | bytes 9437188
  29.9 225.3 %all-gather.9.cloned.1.call-start = ((), (), s32[]{:S(2)}) async-start(), calls=%async_computation.1 | async-start | bytes 2359296 | tf_op jit(solution)/shard_map/all_gather | solution.py:22
  30.7 270.2 %all-gather.7.cloned.1.call-start = ((), (), s32[]{:S(2)}) async-start(), calls=%async_computation | async-start | bytes 2359296 | tf_op jit(solution)/shard_map/all_gather | solution.py:22
  300.9 3.2 %copy-start.3 = (f32[1,2,32,1024]{3,2,1,0:T(8,128)S(1)}, f32[1,2,32,1024]{3,2,1,0:T(8,128)}, u32[]{:S(2)}) copy-start(f32[1,2,32,1024]{3,2,1,0:T(8,128)} %dynamic-slice_bitcast_fusion.1) | copy-start | bytes 786436
  304.0 1.5 copy-start.1
  304.0 1.8 copy-start.2
Sparse Core Ops, SparseCore 0:
  9.8 47.1 all-gather.10
  60.5 149.7 all-reduce.2
  212.0 43.1 all-gather.8
  257.5 43.3 all-gather.6
where the time goes:
time: 315 us; the launch traced here: 314 us
  waiting for transfers between devices  262 us (83%)
  other arithmetic  19.9 us (6%)
  between operations  15.2 us (5%)
  blocking collectives  13.1 us (4%)
  local copies, waits for them, and re-layouts  3.61 us (1%)
    psum x1, waiting for transfers between devices, on_device(): pseudo = lax.psum(term, 'replica')  153 us
    all_gather x3, waiting for transfers between devices, on_device(): moment_full = lax.all_gather(momentum[layer], 'replica', axis=1, tiled=True)  108 us
    psum x1, blocking collectives, on_device(): total = lax.psum(counts[0], 'replica').astype(jnp.float32)  13.1 us
    add x3, other arithmetic, on_device(): moment_next = momentum_rate * moment_full + pseudo  10.8 us
  transfers between devices with their start and end apart: 4, of which 4 were waited for; matrix products, arithmetic and copies ran while one was open for 5% of the time, Pallas kernels for 0%

commit v1 on v0

--- a/solution.py
+++ b/solution.py
@@ -18,7 +18,7 @@
     for layer in range(LAYERS):
         base = anchor[layer].astype(jnp.float32)
         term = share * (base - inner[0, layer].astype(jnp.float32))
-        pseudo = lax.psum(term, "replica")
+        pseudo = lax.all_gather(term, axis_name="replica").sum(axis=0)
         moment_full = lax.all_gather(momentum[layer], "replica", axis=1, tiled=True)
         moment_next = momentum_rate * moment_full + pseudo
         weights_next = (base - outer_rate * (pseudo + momentum_rate * moment_next)).astype(

time: 315 us -> 699 us (2.22)
  waiting for transfers between devices: 262 us -> 619 us
  other arithmetic: 19.9 us -> 47.9 us
    all_gather x0 -> x3, waiting for transfers between devices: none -> 499 us  [on_device(): pseudo = lax.all_gather(term, axis_name='replica').sum(axis=0)]
    psum x1 -> x0, waiting for transfers between devices: 153 us -> none  [on_device(): pseudo = lax.psum(term, 'replica')]
    reduce_sum x0 -> x3, other arithmetic: none -> 27.9 us  [on_device(): pseudo = lax.all_gather(term, axis_name='replica').sum(axis=0)]
    all_gather x3, waiting for transfers between devices: 108 us -> 118 us  [on_device(): moment_full = lax.all_gather(momentum[layer], 'replica', axis=1, tiled=True)]
  transfers between devices with their start and end apart: 4 -> 6, of which waited for: 4 -> 6; matrix products, arithmetic and copies ran while one was open for 5% -> 5% of each run, Pallas kernels for 0% -> 0%
where the time goes in v1:
time: 699 us; the launch traced here: 698 us
  waiting for transfers between devices  619 us (89%)
  other arithmetic  47.9 us (7%)
  between operations  15.5 us (2%)
  blocking collectives  13 us (2%)
    all_gather x3, waiting for transfers between devices, on_device(): pseudo = lax.all_gather(term, axis_name='replica').sum(axis=0)  499 us
    all_gather x3, waiting for transfers between devices, on_device(): moment_full = lax.all_gather(momentum[layer], 'replica', axis=1, tiled=True)  118 us
    reduce_sum x3, other arithmetic, on_device(): pseudo = lax.all_gather(term, axis_name='replica').sum(axis=0)  27.9 us
  transfers between devices with their start and end apart: 6, of which 6 were waited for; matrix products, arithmetic and copies ran while one was open for 5% of the time, Pallas kernels for 0%

profile of v1, /device:TPU:8, one launch (start us, length us, event | category | flops | bytes accessed | tf_op | source)
XLA Modules:
  0.0 698.4 jit_solution(35592414746616576)
XLA Ops:
  7.2 0.0 all-gather.14.cloned.1.call-start
  7.9 13.0 %psum.7 = s32[]{:T(128)} all-reduce(s32[]{:T(128)} %bitcast.1), channel_id=1, replica_groups=mesh['replica'=8,'fsdp'=32] {'replica'}, use_global_device_ids=true, to_apply=%region_0.0 | all-reduce | flops 1 | bytes 8 | tf_op jit(solution)/shard_map/psum | solution.py:12
  21.6 6.2 fusion.2
  27.8 0.0 all-gather.14.cloned.1.call-update
  27.8 0.0 all-gather.12.cloned.1.call-start
  27.9 0.0 copy-start.4
  27.9 0.7 all-gather.12.cloned.1.call-update
  28.6 0.0 all-gather.10.cloned.1.call-start
  28.6 0.7 all-gather.10.cloned.1.call-update
  29.3 0.0 all-gather.20.cloned.1.call-start
  29.3 0.0 copy-done.4
  29.4 0.9 fusion.12
  30.3 0.0 all-gather.20.cloned.1.call-update
  30.3 0.0 all-gather.18.cloned.1.call-start
  30.3 0.5 all-gather.18.cloned.1.call-update
  30.9 0.0 all-gather.16.cloned.1.call-start
  30.9 0.5 all-gather.16.cloned.1.call-update
  31.4 169.7 %all-gather.14.cloned.1.call-done = f32[8,2,256,1024]{3,2,1,0:T(8,128)} async-done(((f32[1,2,256,1024]{3,2,1,0:T(8,128)}), f32[8,2,256,1024]{3,2,1,0:T(8,128)}) %all-gather.14.cloned.1.call-update) | async-done | bytes 16777232 | tf_op jit(solution)/shard_map/all_gather | solution.py:21
  201.2 9.4 %reduce_sum.29 = f32[2,256,1024]{2,1,0:T(8,128)} reduce(f32[8,2,256,1024]{3,2,1,0:T(8,128)} %all-gather.14.cloned.1.call-done, f32[]{:T(128)} %constant.2.clone.1), dimensions={0}, to_apply=%region_3.0 | reduce | flops 3670016 | bytes 18874372 | tf_op jit(solution)/shard_map/reduce_sum | solution.py:21
  210.5 164.4 %all-gather.12.cloned.1.call-done = f32[8,2,256,1024]{3,2,1,0:T(8,128)} async-done(((f32[1,2,256,1024]{3,2,1,0:T(8,128)}), f32[8,2,256,1024]{3,2,1,0:T(8,128)}) %all-gather.12.cloned.1.call-update) | async-done | bytes 16777232 | tf_op jit(solution)/shard_map/all_gather | solution.py:21
  374.9 9.3 %reduce_sum.28 = f32[2,256,1024]{2,1,0:T(8,128)} reduce(f32[8,2,256,1024]{3,2,1,0:T(8,128)} %all-gather.12.cloned.1.call-done, f32[]{:T(128)} %constant.2.clone.1), dimensions={0}, to_apply=%region_2.0 | reduce | flops 3670016 | bytes 18874372 | tf_op jit(solution)/shard_map/reduce_sum | solution.py:21
  384.2 0.0 copy-start
  384.2 165.0 %all-gather.10.cloned.1.call-done = f32[8,2,256,1024]{3,2,1,0:T(8,128)} async-done(((f32[1,2,256,1024]{3,2,1,0:T(8,128)}), f32[8,2,256,1024]{3,2,1,0:T(8,128)}) %all-gather.10.cloned.1.call-update) | async-done | bytes 16777232 | tf_op jit(solution)/shard_map/all_gather | solution.py:21
  549.2 9.3 %reduce_sum.27 = f32[2,256,1024]{2,1,0:T(8,128)} reduce(f32[8,2,256,1024]{3,2,1,0:T(8,128)} %all-gather.10.cloned.1.call-done, f32[]{:T(128)} %constant.2.clone.1), dimensions={0}, to_apply=%region_1.0 | reduce | flops 3670016 | bytes 18874372 | tf_op jit(solution)/shard_map/reduce_sum | solution.py:21
  558.5 35.5 %all-gather.20.cloned.1.call-done = f32[1,2,256,1024]{3,2,1,0:T(8,128)} async-done(((f32[1,2,32,1024]{3,2,1,0:T(8,128)}), f32[1,2,256,1024]{3,2,1,0:T(8,128)}) %all-gather.20.cloned.1.call-update) | async-done | bytes 2097168 | tf_op jit(solution)/shard_map/all_gather | solution.py:22
  594.0 0.0 copy-done
  594.0 3.9 bitcast_add_fusion
  597.9 41.1 %all-gather.18.cloned.1.call-done = f32[1,2,256,1024]{3,2,1,0:T(8,128)} async-done(((f32[1,2,32,1024]{3,2,1,0:T(8,128)}), f32[1,2,256,1024]{3,2,1,0:T(8,128)}) %all-gather.18.cloned.1.call-update) | async-done | bytes 2097168 | tf_op jit(solution)/shard_map/all_gather | solution.py:22
  639.0 3.9 bitcast_add_fusion.1
  642.9 0.7 dynamic-slice_bitcast_fusion.1
  643.6 41.0 %all-gather.16.cloned.1.call-done = f32[1,2,256,1024]{3,2,1,0:T(8,128)} async-done(((f32[1,2,32,1024]{3,2,1,0:T(8,128)}), f32[1,2,256,1024]{3,2,1,0:T(8,128)}) %all-gather.16.cloned.1.call-update) | async-done | bytes 2097168 | tf_op jit(solution)/shard_map/all_gather | solution.py:22
  684.7 0.0 copy-start.3
  684.7 3.1 bitcast_add_fusion.2
  687.8 0.0 copy-start.1
  687.8 0.0 copy-start.2
  687.8 0.0 copy-done.3
  687.8 0.9 pad_maximum_fusion.1
  688.8 0.5 copy-done.1
  689.3 0.3 copy-done.2
  689.6 2.0 pad_maximum_fusion
  (2 shorter events, 0.0 us)
Async XLA Ops:
  7.2 194.0 %all-gather.14.cloned.1.call-start = ((), (), s32[]{:S(2)}) async-start(), calls=%async_computation.2 | async-start | bytes 18874368 | tf_op jit(solution)/shard_map/all_gather | solution.py:21
  27.8 347.1 %all-gather.12.cloned.1.call-start = ((), (), s32[]{:S(2)}) async-start(), calls=%async_computation.1 | async-start | bytes 18874368 | tf_op jit(solution)/shard_map/all_gather | solution.py:21
  27.9 1.5 copy-start.4
  28.6 520.7 %all-gather.10.cloned.1.call-start = ((), (), s32[]{:S(2)}) async-start(), calls=%async_computation | async-start | bytes 18874368 | tf_op jit(solution)/shard_map/all_gather | solution.py:21
  29.3 564.7 %all-gather.20.cloned.1.call-start = ((), (), s32[]{:S(2)}) async-start(), calls=%async_computation.5 | async-start | bytes 2359296 | tf_op jit(solution)/shard_map/all_gather | solution.py:22
  30.3 608.8 %all-gather.18.cloned.1.call-start = ((), (), s32[]{:S(2)}) async-start(), calls=%async_computation.4 | async-start | bytes 2359296 | tf_op jit(solution)/shard_map/all_gather | solution.py:22
  30.9 653.8 %all-gather.16.cloned.1.call-start = ((), (), s32[]{:S(2)}) async-start(), calls=%async_computation.3 | async-start | bytes 2359296 | tf_op jit(solution)/shard_map/all_gather | solution.py:22
  384.2 209.8 %copy-start = (bf16[3,2,256,1024]{3,2,1,0:T(8,128)(2,1)S(1)}, bf16[3,2,256,1024]{3,2,1,0:T(8,128)(2,1)}, u32[]{:S(2)}) copy-start(bf16[3,2,256,1024]{3,2,1,0:T(8,128)(2,1)} %param.6) | copy-start | bytes 9437188
  684.7 3.2 copy-start.3
  687.8 1.5 copy-start.1
  687.8 1.8 copy-start.2
Sparse Core Ops, SparseCore 0:
  27.9 173.2 all-gather.13
  203.0 171.8 all-gather.11
  377.3 171.8 all-gather.9
  550.9 43.0 all-gather.19
  595.6 43.3 all-gather.17
  641.3 43.3 all-gather.15
